TPU v7x, 32 devices: a whole 2x2x4 slice. The times are simulated.
32 devices in a mesh: rows: 4 (over z), cols: 8 (over y, x, core).
Axes of the slice: x: 2, y: 2, z: 4, core: 2. Of those that a mesh axis runs over, the one named last changes fastest.
Arguments:
- left_fine: bfloat16 [128, 1024, 128], P('rows', 'cols'), may hold values from -40 to 40
- right_fine: bfloat16 [128, 1024, 128], P('rows', 'cols'), may hold values from -40 to 40
- left_coarse: bfloat16 [32, 256, 128], P('rows', 'cols'), may hold values from -40 to 40
- right_coarse: bfloat16 [32, 256, 128], P('rows', 'cols'), may hold values from -40 to 40
- candidates: int32 [8, 32, 4], P(None, 'rows'), may hold values from 0 to 7, all different within a row; in each aligned block of 8 rows (0 to 7, 8 to 15, ..., all dimensions but the last counted through in order) at most 8 rows name the same one
- counts: int32 [8, 32], P(None, 'rows'), may hold values from 1 to 4
- query_weight: bfloat16 [128, 128], replicated, may hold values from -1 to 1
- key_weight: bfloat16 [128, 128], replicated, may hold values from -1 to 1
- value_weight: bfloat16 [128, 128], replicated, may hold values from -0.5 to 0.5
- out_weight: bfloat16 [128, 128], replicated, may hold values from -0.5 to 0.5
- norm_gain: float32 [128], replicated, may hold values from 0.5 to 1.5
Outputs:
- fine_features: bfloat16 [128, 1024, 128], P('rows', 'cols')
- coarse_prior: bfloat16 [32, 256, 128], P('rows', 'cols')
Inputs may be any that keep to these rules, and one draw needn't show every extreme that they name: `candidates`: each list names 4 different right blocks; entries at k >= counts are not used. For one left block, within the 8 bands of one index of rows (aligned groups of bands), no right block is named more than 8 times, and in some groups one is named exactly 8 times.
All inputs are finite; a program needn't handle non-finite values.
Results may differ from a plain program's by a relative error of at most 0.01.
Values may be sent and summed in bfloat16 or wider, within the bound.
A program may use at most 192 MiB of HBM per device.

v0:
```python
import functools
import math

import jax
import jax.numpy as jnp
import numpy as np
from jax import lax
from jax.experimental import pallas as pl
from jax.experimental.pallas import tpu as pltpu
from jax.sharding import PartitionSpec as P

HEADS = 8
HEAD_DIM = 16
BLOCK = 128
BAND = 4
EPSILON = 1e-05
PAIRS = HEADS // 2
EDGE = 16
EARLY = 6
LEAD = 4
MESH = pl.DeviceIdType.MESH
KEY_SCALE = math.log2(math.e) / math.sqrt(HEAD_DIM)
BF16 = jnp.bfloat16
F32 = jnp.float32


def nt(a, b):
    return lax.dot_general(a, b, (((1,), (1,)), ((), ())), preferred_element_type=F32)


def tn(a, b):
    return lax.dot_general(a, b, (((0,), (0,)), ((), ())), preferred_element_type=F32)


def nn(a, b):
    return jnp.dot(a, b, preferred_element_type=F32)


def layer_norm(values, norm_gain):
    average = jnp.mean(values, axis=-1, keepdims=True)
    centred = values - average
    spread = jnp.mean(centred * centred, axis=-1, keepdims=True)
    return centred * lax.rsqrt(spread + EPSILON) * norm_gain


def upsample_matrix(cols):
    taps = np.array(
        [[0.375, 0.625, 0.0], [0.125, 0.875, 0.0], [0.0, 0.875, 0.125], [0.0, 0.625, 0.375]]
    )
    pitch = cols + 2 * EDGE
    out = np.zeros((BAND, cols, 4, 3, pitch), np.float32)
    for c in range(cols):
        for t in range(4):
            for d in range(3):
                out[:, c, t, :, c + d + EDGE - 1] = taps[:, :] * taps[t, d]
    return out.reshape(BAND * cols * 4, 3 * pitch)


def project_blocks(blocks, wkv_ref):
    feat = blocks[0].shape[1]
    keys, values = [], []
    for block in blocks:
        both = nn(block, wkv_ref[...])
        keys.append((both[:, :feat] * KEY_SCALE).astype(BF16))
        values.append(both[:, feat:].astype(BF16).T)
    return jnp.concatenate(keys, axis=0), jnp.concatenate(values, axis=1)


def attend(keys, values, ones, spread_ref):
    parts = []
    width = spread_ref.shape[1] // HEADS

    def score(pair):
        return nn(keys, spread_ref[:, pair * 2 * width : (pair + 1) * 2 * width])

    ahead = score(0)
    for pair in range(PAIRS):
        scores = ahead
        if pair + 1 < PAIRS:
            ahead = score(pair + 1)
        top = jnp.max(scores, axis=0, keepdims=True)
        weights = jnp.exp2((scores - top).astype(BF16))
        rows = values[pair * 2 * HEAD_DIM : (pair + 1) * 2 * HEAD_DIM]
        mix = nn(jnp.concatenate([rows, ones], axis=0), weights)
        inverse = 1.0 / mix[2 * HEAD_DIM : 2 * HEAD_DIM + 1]
        parts.append(mix[:HEAD_DIM, :width] * inverse[:, :width])
        parts.append(mix[HEAD_DIM : 2 * HEAD_DIM, width:] * inverse[:, width:])
    return jnp.concatenate(parts, axis=0).astype(BF16)


def query_stage(left, coarse, up_ref, wq_ref):
    up = nn(up_ref[...], coarse)
    query_in = (left.reshape(up.shape).astype(F32) + up).astype(BF16)
    return query_in, nt(wq_ref[...], query_in).astype(BF16)


def spread_queries(query_ref, spread_ref, start):
    for h in range(HEADS):
        rows = slice(h * HEAD_DIM, (h + 1) * HEAD_DIM)
        spread_ref[rows, h * BLOCK : (h + 1) * BLOCK] = query_ref[rows, pl.ds(start, BLOCK)]


def out_stage(query_in, mixed, wo_ref, gain_ref):
    product = tn(mixed, wo_ref[...])
    return layer_norm(query_in.astype(F32) + product, gain_ref[...]).astype(BF16)


def flipped(index, bit):
    return index + bit - 2 * bit * ((index // bit) % 2)


def gather_hops(n, me):
    if n != 8:
        return [(me, (me + j) % n, (me + n - j) % n, None) for j in range(1, n)]
    a, b, c = flipped(me, 1), flipped(me, 2), flipped(me, 4)
    d = flipped(b, 4)
    odd = me % 2
    relay_block = b + odd * (c - b)
    relay_target = c + odd * (b - c)
    return [
        (me, b, b, None),
        (me, c, c, None),
        (me, a, a, None),
        (relay_block, relay_target, d, (0, 1)),
        (b, a, flipped(b, 1), (0,)),
        (c, a, flipped(c, 1), (1,)),
        (d, a, flipped(d, 1), (3,)),
    ]


def gather_kernel(
    list_ref,
    count_ref,
    left_ref,
    right_ref,
    left_coarse_ref,
    right_coarse_ref,
    up_ref,
    wq_ref,
    wkv_ref,
    wo_ref,
    gain_ref,
    fold_ref,
    late_ref,
    fine_ref,
    prior_ref,
    ext_ref,
    *scratch,
    n,
    row_devices,
    early,
    length,
):
    bands_ref = scratch[:early]
    (
        coarse_ref,
        edge_low_ref,
        edge_high_ref,
        rows_ref,
        query_ref,
        spread_ref,
        mix_ref,
        coarse_send,
        coarse_recv,
        edge_send,
        edge_recv,
        fine_send,
        fine_recv,
        local_sem,
    ) = scratch[early:]
    me = lax.axis_index("cols")
    row = lax.axis_index("rows")
    bands = right_ref.shape[0] // BAND
    coarse_rows, coarse_cols, feat = left_coarse_ref.shape
    hops = gather_hops(n, me)

    barrier = pltpu.get_barrier_semaphore()
    for j in range(1, n):
        pl.semaphore_signal(
            barrier, inc=1, device_id={"cols": (me + j) % n}, device_id_type=MESH
        )

    @pl.when(row > 0)
    def _():
        pl.semaphore_signal(barrier, inc=1, device_id={"rows": row - 1}, device_id_type=MESH)

    @pl.when(row < row_devices - 1)
    def _():
        pl.semaphore_signal(barrier, inc=1, device_id={"rows": row + 1}, device_id_type=MESH)

    inner = (row > 0).astype(jnp.int32) + (row < row_devices - 1).astype(jnp.int32)
    pl.semaphore_wait(barrier, n - 1 + inner)

    def coarse_copy(j):
        return pltpu.make_async_remote_copy(
            src_ref=right_coarse_ref,
            dst_ref=coarse_ref.at[me],
            send_sem=coarse_send.at[j - 1],
            recv_sem=coarse_recv.at[j - 1],
            device_id={"cols": (me + j) % n},
            device_id_type=MESH,
        )

    def place(g, block):
        if g < early:
            return bands_ref[g].at[block]
        return late_ref.at[block, pl.ds((g - early) * BAND, BAND)]

    def fine_copy(g, hop):
        block, target, _, after = hops[hop]
        if after is None:
            source = right_ref.at[pl.ds(g * BAND, BAND)]
        else:
            source = place(g, block)
        return pltpu.make_async_remote_copy(
            src_ref=source,
            dst_ref=place(g, block),
            send_sem=fine_send.at[g, hop],
            recv_sem=fine_recv.at[g, hop],
            device_id={"cols": target},
            device_id_type=MESH,
        )

    def own_copy(g):
        return pltpu.make_async_copy(
            right_ref.at[pl.ds(g * BAND, BAND)], place(g, me), local_sem.at[g]
        )

    arrived = [set() for _ in range(bands)]

    def take(g, hop):
        if hop not in arrived[g]:
            arrived[g].add(hop)
            fine_copy(g, hop).wait_recv()

    levels = []
    for hop in hops:
        levels.append(0 if hop[3] is None else 1 + max(levels[i] for i in hop[3]))
    depth = max(levels)

    def send(g, level):
        for hop in range(len(hops)):
            if levels[hop] == level:
                for needed in hops[hop][3] or ():
                    take(g, needed)
                fine_copy(g, hop).start()

    ticks = []
    for t in range(1, bands + depth):
        ticks.append(
            [(t - level, level) for level in range(depth, 0, -1) if 0 <= t - level < bands]
            + ([(t + LEAD - 1, 0)] if t + LEAD - 1 < bands else [])
        )

    def tick():
        if ticks:
            for g, level in ticks.pop(0):
                send(g, level)

    for j in range(1, n):
        coarse_copy(j).start()
    for g in range(bands):
        own_copy(g).start()
    for g in range(min(LEAD, bands)):
        send(g, 0)

    spread_ref[...] = jnp.zeros_like(spread_ref)
    coarse_ref[me] = right_coarse_ref[...]
    for j in range(1, n):
        coarse_copy(j).wait()

    wide = HEADS * coarse_cols
    diagonal = (
        lax.broadcasted_iota(jnp.int32, (feat, wide), 0) // HEAD_DIM
        == lax.broadcasted_iota(jnp.int32, (feat, wide), 1) // coarse_cols
    )

    def coarse_row(r, carry):
        right = coarse_ref[:, r].reshape(n * coarse_cols, feat)
        left = left_coarse_ref[r]
        keys, values = project_blocks([right], wkv_ref)
        queries = nt(wq_ref[...], jnp.concatenate([left] * HEADS, axis=0))
        queries = jnp.where(diagonal, queries, 0.0).astype(BF16)
        scores = nn(keys, queries)
        top = jnp.max(scores, axis=0, keepdims=True)
        weights = jnp.exp2((scores - top).astype(BF16))
        total = jnp.sum(weights.astype(F32), axis=0, keepdims=True)
        mixed = nn(values, weights) * (1.0 / total)
        mixed = jnp.where(diagonal, mixed, 0.0).astype(BF16)
        folded = nt(fold_ref[...], mixed).astype(BF16)
        out = left.astype(F32) + nn(folded, wo_ref[...])
        out = layer_norm(out, gain_ref[...]).astype(BF16)
        rows_ref[r + 1] = out
        prior_ref[r] = out
        return carry

    lax.fori_loop(0, coarse_rows // 2, coarse_row, 0)
    tick()
    lax.fori_loop(coarse_rows // 2, coarse_rows, coarse_row, 0)

    def row_copy(up):
        return pltpu.make_async_remote_copy(
            src_ref=prior_ref.at[0 if up else coarse_rows - 1],
            dst_ref=rows_ref.at[coarse_rows + 1 if up else 0],
            send_sem=edge_send.at[0 if up else 1],
            recv_sem=edge_recv.at[0 if up else 1],
            device_id={"rows": row - 1 if up else row + 1},
            device_id_type=MESH,
        )

    def col_copy(left):
        return pltpu.make_async_remote_copy(
            src_ref=rows_ref.at[:, pl.ds(0 if left else coarse_cols - EDGE, EDGE)],
            dst_ref=edge_high_ref if left else edge_low_ref,
            send_sem=edge_send.at[2 if left else 3],
            recv_sem=edge_recv.at[2 if left else 3],
            device_id={"cols": me - 1 if left else me + 1},
            device_id_type=MESH,
        )

    has = (row > 0, row < row_devices - 1, me > 0, me < n - 1)

    @pl.when(has[0])
    def _():
        row_copy(True).start()

    @pl.when(has[1])
    def _():
        row_copy(False).start()

    @pl.when(has[0])
    def _():
        row_copy(False).wait_recv()
        row_copy(True).wait_send()

    @pl.when(jnp.logical_not(has[0]))
    def _():
        rows_ref[0] = rows_ref[1]

    @pl.when(has[1])
    def _():
        row_copy(True).wait_recv()
        row_copy(False).wait_send()

    @pl.when(jnp.logical_not(has[1]))
    def _():
        rows_ref[coarse_rows + 1] = rows_ref[coarse_rows]

    @pl.when(has[2])
    def _():
        col_copy(True).start()

    @pl.when(has[3])
    def _():
        col_copy(False).start()

    tick()

    @pl.when(has[2])
    def _():
        col_copy(False).wait_recv()
        col_copy(True).wait_send()

    @pl.when(jnp.logical_not(has[2]))
    def _():
        edge_low_ref[...] = jnp.broadcast_to(rows_ref[:, 0:1], edge_low_ref.shape)

    @pl.when(has[3])
    def _():
        col_copy(True).wait_recv()
        col_copy(False).wait_send()

    @pl.when(jnp.logical_not(has[3]))
    def _():
        edge_high_ref[...] = jnp.broadcast_to(
            rows_ref[:, coarse_cols - 1 : coarse_cols], edge_high_ref.shape
        )

    ext_ref[:, :EDGE] = edge_low_ref[...]
    ext_ref[:, EDGE : EDGE + coarse_cols] = rows_ref[...]
    ext_ref[:, EDGE + coarse_cols :] = edge_high_ref[...]

    for g in range(early):
        if g == 0:
            tick()
        own_copy(g).wait()
        for hop in range(len(hops)):
            take(g, hop)
        coarse = jnp.concatenate([ext_ref[g + i] for i in range(3)], axis=0)
        query_in, queries = query_stage(left_ref[g * BAND : (g + 1) * BAND], coarse, up_ref, wq_ref)
        query_ref[...] = queries
        used = count_ref[g]
        picks = [
            jnp.where(k < used, list_ref[g * length + k], list_ref[g * length])
            for k in range(length)
        ]
        lanes = lax.broadcasted_iota(jnp.int32, (1, length * BLOCK), 1)
        live = jnp.where(lanes < used * BLOCK, 1.0, 0.0).astype(BF16)

        def fine_row(r, carry, g=g, picks=picks, live=live):
            keys, values = project_blocks(
                [bands_ref[g][picks[k], r] for k in range(length)], wkv_ref
            )
            values = values * live
            ones = jnp.broadcast_to(live, (HEAD_DIM, live.shape[1]))
            start = pl.multiple_of(r * BLOCK, BLOCK)
            spread_queries(query_ref, spread_ref, start)
            mix_ref[:, pl.ds(start, BLOCK)] = attend(keys, values, ones, spread_ref)
            return carry

        lax.fori_loop(0, BAND // 2, fine_row, 0)
        tick()
        lax.fori_loop(BAND // 2, BAND, fine_row, 0)
        out = out_stage(query_in, mix_ref[...], wo_ref, gain_ref)
        fine_ref[g * BAND : (g + 1) * BAND] = out.reshape(BAND, BLOCK, feat)

    while ticks:
        tick()
    for g in range(bands):
        if g >= early:
            own_copy(g).wait()
        for hop in range(len(hops)):
            take(g, hop)
            fine_copy(g, hop).wait_send()


def gather_stage(mesh_rows, n, left_fine, right_fine, left_coarse, right_coarse, lists, counts, w):
    rows, cols, feat = left_fine.shape
    bands = rows // BAND
    early = min(EARLY, bands - 1)
    coarse_rows, coarse_cols, _ = left_coarse.shape
    fold = np.tile(np.eye(coarse_cols, dtype=np.float32), (1, HEADS))
    hop_count = len(gather_hops(n, 0))
    vmem = pl.BlockSpec(memory_space=pltpu.VMEM)
    smem = pl.BlockSpec(memory_space=pltpu.SMEM)
    return pl.pallas_call(
        functools.partial(
            gather_kernel, n=n, row_devices=mesh_rows, early=early, length=lists.shape[1]
        ),
        out_shape=(
            jax.ShapeDtypeStruct((n, (bands - early) * BAND, cols, feat), BF16),
            jax.ShapeDtypeStruct((early * BAND, cols, feat), BF16),
            jax.ShapeDtypeStruct(left_coarse.shape, BF16),
            jax.ShapeDtypeStruct((coarse_rows + 2, coarse_cols + 2 * EDGE, feat), BF16),
        ),
        in_specs=[smem, smem] + [vmem] * 10,
        out_specs=(pl.BlockSpec(memory_space=pl.ANY), vmem, vmem, vmem),
        scratch_shapes=[pltpu.VMEM((n, BAND, cols, feat), BF16) for _ in range(early)]
        + [
            pltpu.VMEM((n,) + right_coarse.shape, BF16),
            pltpu.VMEM((coarse_rows + 2, EDGE, feat), BF16),
            pltpu.VMEM((coarse_rows + 2, EDGE, feat), BF16),
            pltpu.VMEM((coarse_rows + 2, coarse_cols, feat), BF16),
            pltpu.VMEM((feat, BAND * BLOCK), BF16),
            pltpu.VMEM((feat, HEADS * BLOCK), BF16),
            pltpu.VMEM((feat, BAND * BLOCK), BF16),
            pltpu.SemaphoreType.DMA((n - 1,)),
            pltpu.SemaphoreType.DMA((n - 1,)),
            pltpu.SemaphoreType.DMA((4,)),
            pltpu.SemaphoreType.DMA((4,)),
            pltpu.SemaphoreType.DMA((bands, hop_count)),
            pltpu.SemaphoreType.DMA((bands, hop_count)),
            pltpu.SemaphoreType.DMA((bands,)),
        ],
        compiler_params=pltpu.CompilerParams(collective_id=0, has_side_effects=True),
        name="gather_stage",
    )(
        lists.reshape(-1),
        counts,
        left_fine,
        right_fine,
        left_coarse,
        right_coarse,
        w["up"],
        w["wq"],
        w["wkv"],
        w["wo"],
        w["gain"],
        jnp.asarray(fold, BF16),
    )


def fine_kernel(
    list_ref,
    count_ref,
    left_ref,
    ext_ref,
    up_ref,
    wq_ref,
    wkv_ref,
    wo_ref,
    gain_ref,
    done_ref,
    *refs,
    early,
):
    list_length = len(refs) - 4
    cand_refs = refs[:list_length]
    out_ref, query_ref, spread_ref, mix_ref = refs[list_length:]
    band = pl.program_id(0)
    feat = wq_ref.shape[0]

    @pl.when(pl.program_id(0) == 0)
    def _():
        spread_ref[...] = jnp.zeros_like(spread_ref)

    @pl.when(band < early)
    def _():
        out_ref[...] = done_ref[...]

    @pl.when(band >= early)
    def _():
        coarse = jnp.concatenate([ext_ref[band + i] for i in range(3)], axis=0)
        query_in, queries = query_stage(left_ref[...], coarse, up_ref, wq_ref)
        query_ref[...] = queries

        for used in range(1, list_length + 1):

            @pl.when(count_ref[band] == used)
            def _():
                def row(r, carry):
                    keys, values = project_blocks(
                        [cand_refs[k][0, r] for k in range(used)], wkv_ref
                    )
                    ones = jnp.ones((HEAD_DIM, used * BLOCK), BF16)
                    start = pl.multiple_of(r * BLOCK, BLOCK)
                    spread_queries(query_ref, spread_ref, start)
                    mix_ref[:, pl.ds(start, BLOCK)] = attend(keys, values, ones, spread_ref)
                    return carry

                lax.fori_loop(0, BAND, row, 0)

        out_ref[...] = out_stage(query_in, mix_ref[...], wo_ref, gain_ref).reshape(out_ref.shape)


def fine_stage(left_fine, gathered, done, ext, lists, counts, w):
    rows, cols, feat = left_fine.shape
    bands = rows // BAND
    early = bands - gathered.shape[1] // BAND
    length = lists.shape[1]

    def whole(shape):
        return pl.BlockSpec(shape, lambda g, c, n: (0,) * len(shape))

    def picked(k):
        return pl.BlockSpec(
            (1, BAND, cols, feat),
            lambda g, c, n: (c[jnp.maximum(g, early) * length + k], jnp.maximum(g - early, 0), 0, 0),
        )

    def banded(index):
        return pl.BlockSpec((BAND, cols, feat), lambda g, c, n: (index(g), 0, 0))

    names = ("up", "wq", "wkv", "wo", "gain")
    return pl.pallas_call(
        functools.partial(fine_kernel, early=early),
        grid_spec=pltpu.PrefetchScalarGridSpec(
            num_scalar_prefetch=2,
            grid=(bands,),
            in_specs=[banded(lambda g: jnp.maximum(g, early)), whole(ext.shape)]
            + [whole(w[name].shape) for name in names]
            + [banded(lambda g: jnp.minimum(g, early - 1))]
            + [picked(k) for k in range(length)],
            out_specs=banded(lambda g: g),
            scratch_shapes=[
                pltpu.VMEM((feat, BAND * BLOCK), BF16),
                pltpu.VMEM((feat, HEADS * BLOCK), BF16),
                pltpu.VMEM((feat, BAND * BLOCK), BF16),
            ],
        ),
        out_shape=jax.ShapeDtypeStruct(left_fine.shape, BF16),
        name="fine_stage",
    )(
        lists.reshape(-1),
        counts,
        left_fine,
        ext,
        *[w[name] for name in names],
        done,
        *([gathered] * length),
    )


def body(
    left_fine,
    right_fine,
    left_coarse,
    right_coarse,
    candidates,
    counts,
    query_weight,
    key_weight,
    value_weight,
    out_weight,
    norm_gain,
):
    me = lax.axis_index("cols")
    lists = lax.dynamic_index_in_dim(candidates, me, 0, keepdims=False)
    own_counts = lax.dynamic_index_in_dim(counts, me, 0, keepdims=False)
    w = {
        "up": jnp.asarray(upsample_matrix(left_coarse.shape[1]), BF16),
        "wq": query_weight.T,
        "wkv": jnp.concatenate([key_weight, value_weight], axis=1),
        "wo": out_weight,
        "gain": norm_gain.reshape(1, -1),
    }
    gathered, done, coarse_prior, ext = gather_stage(
        lax.axis_size("rows"),
        lax.axis_size("cols"),
        left_fine,
        right_fine,
        left_coarse,
        right_coarse,
        lists,
        own_counts,
        w,
    )
    fine_features = fine_stage(left_fine, gathered, done, ext, lists, own_counts, w)
    return (fine_features, coarse_prior)


def solution(mesh):
    return jax.shard_map(
        body,
        mesh=mesh,
        in_specs=(
            P("rows", "cols", None),
            P("rows", "cols", None),
            P("rows", "cols", None),
            P("rows", "cols", None),
            P(None, "rows", None),
            P(None, "rows"),
            P(),
            P(),
            P(),
            P(),
            P(),
        ),
        out_specs=(P("rows", "cols", None), P("rows", "cols", None)),
        check_vma=False,
    )
```

profile of v0, /device:TPU:0, one launch (start us, length us, event | category | flops | bytes accessed | tf_op | source)
XLA Modules:
  0.0 92.4 jit_solution(6417685429535931118)
XLA Ops:
  0.6 0.0 copy-start
  0.6 1.3 %dynamic-slice_bitcast_fusion.count_ref = s32[8]{0:T(128)} fusion(s32[8,8]{1,0:T(8,128)} %param.18, s32[]{:T(128)S(6)} %select_n.6), kind=kLoop, calls=%fused_computation.2 | loop fusion | bytes 68 | tf_op jit(solution)/shard_map/jit(dynamic_index_in_dim)/squeeze | solution.py:599
  1.9 0.0 copy-done
  1.9 0.1 copy.17
  2.0 0.6 reshape.12.list_ref
  2.6 1.5 %copy.18 = bf16[128,128]{0,1:T(8,128)(2,1)} copy(bf16[128,128]{1,0:T(8,128)(2,1)} %param.19) | data formatting | bytes 65536 | tf_op args[6]
  4.0 0.8 constant_dynamic-update-slice_fusion.1
  4.8 0.8 constant_dynamic-update-slice_fusion.wkv_ref
  5.6 0.0 copy-start.1
  5.6 0.6 copy-done.1
  6.2 70.2 %gather_stage.1 = (bf16[8,8,128,128]{3,2,1,0:T(8,128)(2,1)}, bf16[24,128,128]{2,1,0:T(8,128)(2,1)}, bf16[8,32,128]{2,1,0:T(8,128)(2,1)}, bf16[10,64,128]{2,1,0:T(8,128)(2,1)}) custom-call(s32[32]{0:T(128)} %reshape.12.list_ref, s32[8]{0:T(128)} %dynamic-slice_bitcast_fusion.count_ref, bf16[32,128,128]{2,1,0:T(8,128)(2,1)} %left_ref.3, ...), custom_call_target="tpu_custom_call" | custom-call | tf_op jit(solution)/shard_map/gather_stage/pallas_call | solution.py:436
  76.4 0.0 copy-start.2
  76.4 15.3 %fine_stage.1 = bf16[32,128,128]{2,1,0:T(8,128)(2,1)} custom-call(s32[32]{0:T(128)} %reshape.12.list_ref, s32[8]{0:T(128)} %dynamic-slice_bitcast_fusion.count_ref, bf16[32,128,128]{2,1,0:T(8,128)(2,1)} %left_ref.3, bf16[10,64,128]{2,1,0:T(8,128)(2,1)} %get-tuple-element.6.ext_ref, bf16[512,192]{1,0:T(8,128)(2,1)} %constant.18.clone.up_ref, ...), custom_call_target="tpu_custom_call" | custom-call | tf_op jit(solution)/shard_map/fine_stage/pallas_call | solution.py:555
  91.7 0.0 copy-done.2
  91.7 0.6 copy.21
  (1 shorter events, 0.0 us)
Async XLA Ops:
  0.6 1.3 %copy-start = (s32[8,8,4]{1,2,0:T(4,128)S(1)}, s32[8,8,4]{1,2,0:T(4,128)}, u32[]{:S(2)}) copy-start(s32[8,8,4]{1,2,0:T(4,128)} %param.17) | copy-start | bytes 3076
  5.6 0.6 copy-start.1
  76.4 15.3 %copy-start.2 = (bf16[8,32,128]{2,1,0:T(8,128)(2,1)S(1)}, bf16[8,32,128]{2,1,0:T(8,128)(2,1)}, u32[]{:S(2)}) copy-start(bf16[8,32,128]{2,1,0:T(8,128)(2,1)} %get-tuple-element.13) | copy-start | bytes 196612
where the time goes:
time: 93.6 us; the launch traced here: 92.4 us
  Pallas kernels  85.5 us (91%)
  local copies, waits for them, and re-layouts  6.19 us (7%)
    pallas_call x1, Pallas kernels, gather_stage(): pl.pallas_call(functools.partial(gather_kernel, n=n, row_devices=mesh_row...  70.2 us
    pallas_call x1, Pallas kernels, fine_stage(): pl.pallas_call(functools.partial(fine_kernel, early=early), grid_spec=plt...  15.3 us
    unnamed x9, local copies, waits for them, and re-layouts  3.5 us

commit v1 on v0

v1 whole, which is shorter than its diff:
```python
import functools
import math

import jax
import jax.numpy as jnp
import numpy as np
from jax import lax
from jax.experimental import pallas as pl
from jax.experimental.pallas import tpu as pltpu
from jax.sharding import PartitionSpec as P

HEADS = 8
HEAD_DIM = 16
BLOCK = 128
BAND = 4
EPSILON = 1e-05
PAIRS = HEADS // 2
EDGE = 16
LEAD = 2
MESH = pl.DeviceIdType.MESH
KEY_SCALE = math.log2(math.e) / math.sqrt(HEAD_DIM)
BF16 = jnp.bfloat16
F32 = jnp.float32


def nt(a, b):
    return lax.dot_general(a, b, (((1,), (1,)), ((), ())), preferred_element_type=F32)


def tn(a, b):
    return lax.dot_general(a, b, (((0,), (0,)), ((), ())), preferred_element_type=F32)


def nn(a, b):
    return jnp.dot(a, b, preferred_element_type=F32)


def layer_norm(values, norm_gain):
    average = jnp.mean(values, axis=-1, keepdims=True)
    centred = values - average
    spread = jnp.mean(centred * centred, axis=-1, keepdims=True)
    return centred * lax.rsqrt(spread + EPSILON) * norm_gain


def upsample_matrix(cols):
    taps = np.array(
        [[0.375, 0.625, 0.0], [0.125, 0.875, 0.0], [0.0, 0.875, 0.125], [0.0, 0.625, 0.375]]
    )
    pitch = cols + 2 * EDGE
    out = np.zeros((BAND, cols, 4, 3, pitch), np.float32)
    for c in range(cols):
        for t in range(4):
            for d in range(3):
                out[:, c, t, :, c + d + EDGE - 1] = taps[:, :] * taps[t, d]
    return out.reshape(BAND * cols * 4, 3 * pitch)


def project_row(blocks, wk, wv_t):
    block = jnp.concatenate(blocks, axis=0)
    keys = (nn(block, wk) * KEY_SCALE).astype(BF16)
    return keys, nt(wv_t, block).astype(BF16)


def mix_pair(weights, rows, ones):
    width = weights.shape[1] // 2
    mix = nn(jnp.concatenate([rows, ones], axis=0), weights)
    inverse = 1.0 / mix[2 * HEAD_DIM : 2 * HEAD_DIM + 1]
    return [
        mix[:HEAD_DIM, :width] * inverse[:, :width],
        mix[HEAD_DIM : 2 * HEAD_DIM, width:] * inverse[:, width:],
    ]


def query_stage(left, coarse, up_ref, wq_ref):
    up = nn(up_ref[...], coarse)
    query_in = (left.reshape(up.shape).astype(F32) + up).astype(BF16)
    return query_in, nt(wq_ref[...], query_in).astype(BF16)


def spread_queries(query_ref, spread_ref, start):
    for h in range(HEADS):
        rows = slice(h * HEAD_DIM, (h + 1) * HEAD_DIM)
        spread_ref[rows, h * BLOCK : (h + 1) * BLOCK] = query_ref[rows, pl.ds(start, BLOCK)]


def out_stage(query_in, mixed, wo_ref, gain_ref):
    product = tn(mixed, wo_ref[...])
    return layer_norm(query_in.astype(F32) + product, gain_ref[...]).astype(BF16)


def flipped(index, bit):
    return index + bit - 2 * bit * ((index // bit) % 2)


def gather_hops(n, me):
    if n != 8:
        return [(me, (me + j) % n, (me + n - j) % n, None) for j in range(1, n)]
    a, b, c = flipped(me, 1), flipped(me, 2), flipped(me, 4)
    d = flipped(b, 4)
    odd = me % 2
    relay_block = b + odd * (c - b)
    relay_target = c + odd * (b - c)
    return [
        (me, b, b, None),
        (me, c, c, None),
        (me, a, a, None),
        (relay_block, relay_target, d, (0, 1)),
        (b, a, flipped(b, 1), (0,)),
        (c, a, flipped(c, 1), (1,)),
        (d, a, flipped(d, 1), (3,)),
    ]


def gather_kernel(
    list_ref,
    count_ref,
    left_ref,
    right_ref,
    left_coarse_ref,
    right_coarse_ref,
    up_ref,
    wq_in_ref,
    wk_ref,
    wv_ref,
    wo_ref,
    gain_ref,
    fold_ref,
    fine_ref,
    prior_ref,
    *scratch,
    n,
    row_devices,
):
    bands = right_ref.shape[0] // BAND
    length = list_ref.shape[2]
    bands_ref = scratch[:bands]
    (
        ext_ref,
        wq_ref,
        wv_t_ref,
        score_low_ref,
        score_high_ref,
        top_ref,
        key_ref,
        value_ref,
        input_ref,
        coarse_ref,
        edge_low_ref,
        edge_high_ref,
        rows_ref,
        query_ref,
        spread_ref,
        mix_ref,
        coarse_send,
        coarse_recv,
        edge_send,
        edge_recv,
        fine_send,
        fine_recv,
        local_sem,
    ) = scratch[bands:]
    me = lax.axis_index("cols")
    row = lax.axis_index("rows")
    coarse_rows, coarse_cols, feat = left_coarse_ref.shape
    hops = gather_hops(n, me)

    barrier = pltpu.get_barrier_semaphore()
    for j in range(1, n):
        pl.semaphore_signal(
            barrier, inc=1, device_id={"cols": (me + j) % n}, device_id_type=MESH
        )

    @pl.when(row > 0)
    def _():
        pl.semaphore_signal(barrier, inc=1, device_id={"rows": row - 1}, device_id_type=MESH)

    @pl.when(row < row_devices - 1)
    def _():
        pl.semaphore_signal(barrier, inc=1, device_id={"rows": row + 1}, device_id_type=MESH)

    inner = (row > 0).astype(jnp.int32) + (row < row_devices - 1).astype(jnp.int32)
    pl.semaphore_wait(barrier, n - 1 + inner)

    def coarse_copy(j):
        return pltpu.make_async_remote_copy(
            src_ref=right_coarse_ref,
            dst_ref=coarse_ref.at[me],
            send_sem=coarse_send.at[j - 1],
            recv_sem=coarse_recv.at[j - 1],
            device_id={"cols": (me + j) % n},
            device_id_type=MESH,
        )

    def place(g, block):
        return bands_ref[g].at[block]

    def fine_copy(g, hop):
        block, target, _, after = hops[hop]
        if after is None:
            source = right_ref.at[pl.ds(g * BAND, BAND)]
        else:
            source = place(g, block)
        return pltpu.make_async_remote_copy(
            src_ref=source,
            dst_ref=place(g, block),
            send_sem=fine_send.at[g, hop],
            recv_sem=fine_recv.at[g, hop],
            device_id={"cols": target},
            device_id_type=MESH,
        )

    def own_copy(g):
        return pltpu.make_async_copy(
            right_ref.at[pl.ds(g * BAND, BAND)], place(g, me), local_sem.at[g]
        )

    arrived = [set() for _ in range(bands)]

    def take(g, hop):
        if hop not in arrived[g]:
            arrived[g].add(hop)
            fine_copy(g, hop).wait_recv()

    levels = []
    for hop in hops:
        levels.append(0 if hop[3] is None else 1 + max(levels[i] for i in hop[3]))
    depth = max(levels)

    def send(g, level):
        for hop in range(len(hops)):
            if levels[hop] == level:
                for needed in hops[hop][3] or ():
                    take(g, needed)
                fine_copy(g, hop).start()

    sent = set()

    def tick(*steps):
        for g, level in steps:
            if g < bands and level <= depth and (g, level) not in sent:
                sent.add((g, level))
                send(g, level)

    for j in range(1, n):
        coarse_copy(j).start()
    for g in range(bands):
        own_copy(g).start()
    for g in range(LEAD):
        tick((g, 0))

    spread_ref[...] = jnp.zeros_like(spread_ref)
    wq_ref[...] = wq_in_ref[...].T
    wv_t_ref[...] = wv_ref[...].T
    coarse_ref[me] = right_coarse_ref[...]
    for j in range(1, n):
        coarse_copy(j).wait()

    wide = HEADS * coarse_cols
    diagonal = (
        lax.broadcasted_iota(jnp.int32, (feat, wide), 0) // HEAD_DIM
        == lax.broadcasted_iota(jnp.int32, (feat, wide), 1) // coarse_cols
    )

    def coarse_row(r, carry):
        right = coarse_ref[:, r].reshape(n * coarse_cols, feat)
        left = left_coarse_ref[r]
        keys, values = project_row([right], wk_ref[...], wv_t_ref[...])
        queries = nt(wq_ref[...], jnp.concatenate([left] * HEADS, axis=0))
        queries = jnp.where(diagonal, queries, 0.0).astype(BF16)
        scores = nn(keys, queries)
        top = jnp.max(scores, axis=0, keepdims=True)
        weights = jnp.exp2((scores - top).astype(BF16))
        total = jnp.sum(weights.astype(F32), axis=0, keepdims=True)
        mixed = nn(values, weights) * (1.0 / total)
        mixed = jnp.where(diagonal, mixed, 0.0).astype(BF16)
        folded = nt(fold_ref[...], mixed).astype(BF16)
        out = left.astype(F32) + nn(folded, wo_ref[...])
        out = layer_norm(out, gain_ref[...]).astype(BF16)
        rows_ref[r + 1] = out
        prior_ref[r] = out
        return carry

    lax.fori_loop(0, coarse_rows, coarse_row, 0)
    tick((0, 1))

    def row_copy(up):
        return pltpu.make_async_remote_copy(
            src_ref=prior_ref.at[0 if up else coarse_rows - 1],
            dst_ref=rows_ref.at[coarse_rows + 1 if up else 0],
            send_sem=edge_send.at[0 if up else 1],
            recv_sem=edge_recv.at[0 if up else 1],
            device_id={"rows": row - 1 if up else row + 1},
            device_id_type=MESH,
        )

    def col_copy(left):
        return pltpu.make_async_remote_copy(
            src_ref=rows_ref.at[:, pl.ds(0 if left else coarse_cols - EDGE, EDGE)],
            dst_ref=edge_high_ref if left else edge_low_ref,
            send_sem=edge_send.at[2 if left else 3],
            recv_sem=edge_recv.at[2 if left else 3],
            device_id={"cols": me - 1 if left else me + 1},
            device_id_type=MESH,
        )

    has = (row > 0, row < row_devices - 1, me > 0, me < n - 1)

    @pl.when(has[0])
    def _():
        row_copy(True).start()

    @pl.when(has[1])
    def _():
        row_copy(False).start()

    @pl.when(has[0])
    def _():
        row_copy(False).wait_recv()
        row_copy(True).wait_send()

    @pl.when(jnp.logical_not(has[0]))
    def _():
        rows_ref[0] = rows_ref[1]

    @pl.when(has[1])
    def _():
        row_copy(True).wait_recv()
        row_copy(False).wait_send()

    @pl.when(jnp.logical_not(has[1]))
    def _():
        rows_ref[coarse_rows + 1] = rows_ref[coarse_rows]

    @pl.when(has[2])
    def _():
        col_copy(True).start()

    @pl.when(has[3])
    def _():
        col_copy(False).start()

    tick((LEAD, 0), (1, 1), (LEAD + 1, 0))

    @pl.when(has[2])
    def _():
        col_copy(False).wait_recv()
        col_copy(True).wait_send()

    @pl.when(jnp.logical_not(has[2]))
    def _():
        edge_low_ref[...] = jnp.broadcast_to(rows_ref[:, 0:1], edge_low_ref.shape)

    @pl.when(has[3])
    def _():
        col_copy(True).wait_recv()
        col_copy(False).wait_send()

    @pl.when(jnp.logical_not(has[3]))
    def _():
        edge_high_ref[...] = jnp.broadcast_to(
            rows_ref[:, coarse_cols - 1 : coarse_cols], edge_high_ref.shape
        )

    ext_ref[:, :EDGE] = edge_low_ref[...]
    ext_ref[:, EDGE : EDGE + coarse_cols] = rows_ref[...]
    ext_ref[:, EDGE + coarse_cols :] = edge_high_ref[...]

    tick((0, 2))
    scores_ref = (score_low_ref, score_high_ref)

    def arrive(g):
        own_copy(g).wait()
        for hop in range(len(hops)):
            take(g, hop)

    def queries_of(g):
        coarse = jnp.concatenate([ext_ref[g + i] for i in range(3)], axis=0)
        query_in, queries = query_stage(left_ref[g * BAND : (g + 1) * BAND], coarse, up_ref, wq_ref)
        query_ref[g % 2] = queries
        input_ref[g % 2] = query_in

    def picked(g):
        used = count_ref[me, g]
        picks = [
            jnp.where(k < used, list_ref[me, g, k], list_ref[me, g, 0]) for k in range(length)
        ]
        lanes = lax.broadcasted_iota(jnp.int32, (1, length * BLOCK), 1)
        return picks, jnp.where(lanes < used * BLOCK, 1.0, 0.0).astype(BF16)

    def score(pair):
        scores = nn(key_ref[...], spread_ref[:, pair * 2 * BLOCK : (pair + 1) * 2 * BLOCK])
        scores_ref[pair % 2][...] = scores
        top = jnp.max(scores, axis=0, keepdims=True)
        top_ref[pair % 2] = jnp.broadcast_to(top, top_ref.shape[1:])

    def weigh(pair):
        return jnp.exp2((scores_ref[pair % 2][...] - top_ref[pair % 2][0:1]).astype(BF16))

    def open_row(g, r, picks, live):
        keys, values = project_row(
            [bands_ref[g][picks[k], r] for k in range(length)], wk_ref[...], wv_t_ref[...]
        )
        key_ref[...] = keys
        value_ref[...] = values * live
        start = pl.multiple_of(r * BLOCK, BLOCK)
        spread_queries(query_ref.at[g % 2], spread_ref, start)
        score(0)

    def fine_row(g, r, live, follow):
        ones = jnp.broadcast_to(live, (HEAD_DIM, live.shape[1]))
        parts = []
        for pair in range(PAIRS):
            weights = weigh(pair)
            rows = value_ref[pair * 2 * HEAD_DIM : (pair + 1) * 2 * HEAD_DIM]
            if pair + 1 < PAIRS:
                score(pair + 1)
            else:
                follow()
            parts += mix_pair(weights, rows, ones)
        start = pl.multiple_of(r * BLOCK, BLOCK)
        mix_ref[g % 2, :, pl.ds(start, BLOCK)] = jnp.concatenate(parts, axis=0).astype(BF16)

    def finish(g):
        out = out_stage(input_ref[g % 2], mix_ref[g % 2], wo_ref, gain_ref)
        fine_ref[g * BAND : (g + 1) * BAND] = out.reshape(BAND, BLOCK, feat)

    arrive(0)
    queries_of(0)
    picks, live = picked(0)
    open_row(0, 0, picks, live)
    for g in range(bands):
        tick((g + 1, 2), (g + 2, 1), (g + LEAD + 2, 0))

        def inner(r, carry, g=g, picks=picks, live=live):
            fine_row(g, r, live, lambda: open_row(g, r + 1, picks, live))
            return carry

        lax.fori_loop(0, BAND - 1, inner, 0)
        last = live
        if g > 0:
            finish(g - 1)
        if g + 1 < bands:
            arrive(g + 1)
            picks, live = picked(g + 1)
            queries_of(g + 1)
        fine_row(
            g,
            BAND - 1,
            last,
            lambda: open_row(g + 1, 0, picks, live) if g + 1 < bands else None,
        )
    finish(bands - 1)

    for g in range(bands):
        for hop in range(len(hops)):
            fine_copy(g, hop).wait_send()


def fused_stage(mesh_rows, n, left_fine, right_fine, left_coarse, right_coarse, lists, counts, w):
    rows, cols, feat = left_fine.shape
    bands = rows // BAND
    coarse_rows, coarse_cols, _ = left_coarse.shape
    keys = lists.shape[2] * cols
    fold = np.tile(np.eye(coarse_cols, dtype=np.float32), (1, HEADS))
    hop_count = len(gather_hops(n, 0))
    vmem = pl.BlockSpec(memory_space=pltpu.VMEM)
    smem = pl.BlockSpec(memory_space=pltpu.SMEM)
    return pl.pallas_call(
        functools.partial(gather_kernel, n=n, row_devices=mesh_rows),
        out_shape=(
            jax.ShapeDtypeStruct(left_fine.shape, BF16),
            jax.ShapeDtypeStruct(left_coarse.shape, BF16),
        ),
        in_specs=[smem, smem] + [vmem] * 11,
        out_specs=(vmem, vmem),
        scratch_shapes=[pltpu.VMEM((n, BAND, cols, feat), BF16) for _ in range(bands)]
        + [
            pltpu.VMEM((coarse_rows + 2, coarse_cols + 2 * EDGE, feat), BF16),
            pltpu.VMEM((feat, feat), BF16),
            pltpu.VMEM((feat, feat), BF16),
            pltpu.VMEM((keys, 2 * BLOCK), F32),
            pltpu.VMEM((keys, 2 * BLOCK), F32),
            pltpu.VMEM((2, 8, 2 * BLOCK), F32),
            pltpu.VMEM((keys, feat), BF16),
            pltpu.VMEM((feat, keys), BF16),
            pltpu.VMEM((2, BAND * BLOCK, feat), BF16),
            pltpu.VMEM((n,) + right_coarse.shape, BF16),
            pltpu.VMEM((coarse_rows + 2, EDGE, feat), BF16),
            pltpu.VMEM((coarse_rows + 2, EDGE, feat), BF16),
            pltpu.VMEM((coarse_rows + 2, coarse_cols, feat), BF16),
            pltpu.VMEM((2, feat, BAND * BLOCK), BF16),
            pltpu.VMEM((feat, HEADS * BLOCK), BF16),
            pltpu.VMEM((2, feat, BAND * BLOCK), BF16),
            pltpu.SemaphoreType.DMA((n - 1,)),
            pltpu.SemaphoreType.DMA((n - 1,)),
            pltpu.SemaphoreType.DMA((4,)),
            pltpu.SemaphoreType.DMA((4,)),
            pltpu.SemaphoreType.DMA((bands, hop_count)),
            pltpu.SemaphoreType.DMA((bands, hop_count)),
            pltpu.SemaphoreType.DMA((bands,)),
        ],
        compiler_params=pltpu.CompilerParams(collective_id=0, has_side_effects=True),
        name="fused_stage",
    )(
        lists,
        counts,
        left_fine,
        right_fine,
        left_coarse,
        right_coarse,
        jnp.asarray(upsample_matrix(coarse_cols), BF16),
        w["wq"],
        w["wk"],
        w["wv"],
        w["wo"],
        w["gain"],
        jnp.asarray(fold, BF16),
    )


def body(
    left_fine,
    right_fine,
    left_coarse,
    right_coarse,
    candidates,
    counts,
    query_weight,
    key_weight,
    value_weight,
    out_weight,
    norm_gain,
):
    w = {
        "wq": query_weight,
        "wk": key_weight,
        "wv": value_weight,
        "wo": out_weight,
        "gain": norm_gain.reshape(1, -1),
    }
    return fused_stage(
        lax.axis_size("rows"),
        lax.axis_size("cols"),
        left_fine,
        right_fine,
        left_coarse,
        right_coarse,
        candidates,
        counts,
        w,
    )


def solution(mesh):
    return jax.shard_map(
        body,
        mesh=mesh,
        in_specs=(
            P("rows", "cols", None),
            P("rows", "cols", None),
            P("rows", "cols", None),
            P("rows", "cols", None),
            P(None, "rows", None),
            P(None, "rows"),
            P(),
            P(),
            P(),
            P(),
            P(),
        ),
        out_specs=(P("rows", "cols", None), P("rows", "cols", None)),
        check_vma=False,
    )
```

time: 93.6 us -> 75.8 us (0.81); the launches traced: 92.4 us -> 75.5 us
  Pallas kernels: 85.5 us -> 70.4 us
  local copies, waits for them, and re-layouts: 6.19 us -> 4.42 us
    pallas_call x2 -> x1, Pallas kernels: 85.5 us -> 70.4 us  [fused_stage(): pl.pallas_call(functools.partial(gather_kernel, n=n, row_devices=mesh_row...]
    squeeze x1 -> x0, local copies, waits for them, and re-layouts: 1.27 us -> none  [body(): own_counts = lax.dynamic_index_in_dim(counts, me, 0, keepdims=False)]
    unnamed x9 -> x5, local copies, waits for them, and re-layouts: 3.5 us -> 4.42 us
where the time goes in v1:
time: 75.8 us; the launch traced here: 75.5 us
  Pallas kernels  70.4 us (93%)
  local copies, waits for them, and re-layouts  4.42 us (6%)
    pallas_call x1, Pallas kernels, fused_stage(): pl.pallas_call(functools.partial(gather_kernel, n=n, row_devices=mesh_row...  70.4 us
    unnamed x5, local copies, waits for them, and re-layouts  4.42 us

profile of v1, /device:TPU:0, one launch (start us, length us, event | category | flops | bytes accessed | tf_op | source)
XLA Modules:
  0.0 75.5 jit_solution(17289145457680033097)
XLA Ops:
  0.6 1.4 %copy.15.list_ref = s32[8,8,4]{2,1,0:T(8,128)} copy(s32[8,8,4]{1,2,0:T(4,128)} %param.17) | data formatting | bytes 2048 | tf_op args[4]
  2.1 70.4 %fused_stage.1 = (bf16[32,128,128]{2,1,0:T(8,128)(2,1)}, bf16[8,32,128]{2,1,0:T(8,128)(2,1)}) custom-call(s32[8,8,4]{2,1,0:T(8,128)} %copy.15.list_ref, s32[8,8]{1,0:T(8,128)} %count_ref.1, bf16[32,128,128]{2,1,0:T(8,128)(2,1)} %left_ref.1, bf16[32,128,128]{2,1,0:T(8,128)(2,1)} %right_ref.1, bf16[8,32,128]{2,1,0:T(8,128)(2,1)} %left_coarse_ref.1, ...), custom_call_target="tpu_custom_call" | custom-call | tf_op jit(solution)/shard_map/fused_stage/pallas_call | solution.py:468
  72.5 0.0 copy-start
  72.5 2.3 %copy.18 = bf16[32,128,128]{2,1,0:T(8,128)(2,1)} copy(bf16[32,128,128]{2,1,0:T(8,128)(2,1)} %get-tuple-element.4) | data formatting | bytes 2097152
  74.9 0.0 copy-done
  74.9 0.6 copy.19
Async XLA Ops:
  72.5 2.4 %copy-start = (bf16[8,32,128]{2,1,0:T(8,128)(2,1)S(1)}, bf16[8,32,128]{2,1,0:T(8,128)(2,1)}, u32[]{:S(2)}) copy-start(bf16[8,32,128]{2,1,0:T(8,128)(2,1)} %get-tuple-element.5) | copy-start | bytes 196612
